TPU v7x, 32 devices: a whole 2x2x4 slice. The times are simulated.
32 devices in a mesh: sub: 8 (over y, x, core), coarse: 4 (over z).
Axes of the slice: x: 2, y: 2, z: 4, core: 2. Of those that a mesh axis runs over, the one named last changes fastest.
Arguments:
- right_side: float32 [8, 4, 128, 128], P('sub', 'coarse'), may hold values from -150 to 150
- diagonal: float32 [8, 4, 128, 128], P('sub', 'coarse'), may hold values from 2 to 8
- cell_link: float32 [8, 4, 128, 128], P('sub', 'coarse'), may hold values from 0.2 to 0.9
- block_inverse: float32 [8, 4, 128, 128, 128], P('sub', 'coarse'), may hold values from -1 to 1
- coupling: float32 [8, 4, 4, 128, 128], P('sub', 'coarse'), may hold values from -0.26516503 to 0.26516503
- coarse_basis: float32 [8, 4, 128, 128], P('sub', 'coarse'), may hold values from -6 to 6
- coarse_inverse: float32 [512, 512], P('coarse'), may hold values from -0.25 to 0.25
- partner: int32 [8, 4], P('sub'), may hold values from 0 to 7, as said below
- margin_width: int32 [8, 4], P('sub'), may hold values from 4 to 8, as said below
- margin_blocks: int32 [8, 4, 4, 8], P('sub', 'coarse'), may hold values from 0 to 127
- aggregate: int32 [8, 4, 128], P('sub', 'coarse'), may hold values from 0 to 511, as said below
Outputs:
- solution: float32 [8, 4, 128, 128], P('sub', 'coarse')
Inputs may be any that keep to these rules, and one draw needn't show every extreme that they name: partner[s, r] differs from s, partner[partner[s, r], r] = s, and the 4 partners of one subdomain are distinct. margin_width[partner[s, r], r] = margin_width[s, r]; every colour round has a pair with width 8. `margin_blocks`: entries with w >= margin_width[s, r] are not used. aggregate[s, c, b] lies in (s * 4 + c) * 16 to (s * 4 + c + 1) * 16 - 1, and every one of these 16 aggregates has a block of part [s, c].
All inputs are finite; a program needn't handle non-finite values.
Results may differ from a plain program's by a relative error of at most 0.0003.
Values sent between devices are 32-bit elements; how exact they have to be, the bound alone decides.
No kernel may reach another device: no remote copies, remote signals or barrier semaphores. Data moves between devices by JAX's collectives and lax.ppermute only.
A program may use at most 64 MiB of HBM per device.

v0:
```python
import jax
import jax.numpy as jnp
from jax import lax
from jax.sharding import PartitionSpec as P

BS = 128
BPD = 128
AGG_DEV = 16
ITERS = 4


def givens_solve(columns, beta):
    steps_count = len(columns)
    cosines = []
    sines = []
    side_terms = [beta] + [jnp.zeros_like(beta) for unused in range(steps_count)]
    triangle = []
    for column_id in range(steps_count):
        column = list(columns[column_id])
        for row_id in range(column_id):
            upper = column[row_id]
            lower = column[row_id + 1]
            column[row_id] = cosines[row_id] * upper + sines[row_id] * lower
            column[row_id + 1] = cosines[row_id] * lower - sines[row_id] * upper
        upper = column[column_id]
        lower = column[column_id + 1]
        radius = jnp.sqrt(upper * upper + lower * lower)
        cosine = upper / radius
        sine_value = lower / radius
        column[column_id] = radius
        cosines.append(cosine)
        sines.append(sine_value)
        side_terms[column_id + 1] = -sine_value * side_terms[column_id]
        side_terms[column_id] = cosine * side_terms[column_id]
        triangle.append(column)
    weights = [None] * steps_count
    for column_id in reversed(range(steps_count)):
        running = side_terms[column_id]
        for later_col in range(column_id + 1, steps_count):
            running = running - triangle[later_col][column_id] * weights[later_col]
        weights[column_id] = running / triangle[column_id][column_id]
    return weights


def on_device(
    right_side,
    diagonal,
    cell_link,
    block_inverse,
    coupling,
    coarse_basis,
    coarse_inverse,
    partner,
    margin_width,
    margin_blocks,
    aggregate,
):
    highest = lax.Precision.HIGHEST
    block_count = right_side.shape[2]
    unknowns = right_side.shape[3]
    factor = (BS * BPD / AGG_DEV) ** (-0.5)
    inverse_blocks = block_inverse[0, 0]
    couplings = coupling[0, 0]
    basis_local = coarse_basis[0, 0]
    diagonal_local = diagonal[0, 0]
    link_local = cell_link[0, 0]
    paired = partner[0]
    widths = margin_width[0]
    blocks = margin_blocks[0, 0]
    member_of = aggregate[0, 0]
    aggregate_count = coarse_inverse.shape[1]
    member_table = (member_of[:, None] == jnp.arange(aggregate_count)[None, :]).astype(jnp.float32)
    rounds = blocks.shape[0]
    widest = blocks.shape[1]
    target = (blocks.reshape(-1)[:, None] == jnp.arange(block_count)[None, :]).astype(jnp.float32)
    live_mask = (jnp.arange(widest)[None, :] < widths[:, None]).astype(jnp.float32)

    def margin(values):
        outgoing = jnp.take(values, blocks.reshape(-1), axis=0).reshape(rounds, widest, unknowns)
        pieces = []
        for round_id in range(rounds):
            gathered = lax.all_gather(outgoing[round_id], "sub", axis=0, tiled=True)
            pieces.append(lax.dynamic_slice_in_dim(gathered, paired[round_id] * widest, widest, 0))
        incoming = jnp.stack(pieces)
        mapped = (
            jnp.einsum("rij,rwj->rwi", couplings, incoming, precision=highest)
            * live_mask[:, :, None]
        )
        return jnp.einsum(
            "kb,ki->bi", target, mapped.reshape(rounds * widest, unknowns), precision=highest
        )

    def squared_norm(values):
        return lax.psum(jnp.sum(values * values), ("sub", "coarse"))

    start_vector = right_side[0, 0]
    directions = []
    columns = []
    beta = jnp.sqrt(squared_norm(start_vector))
    basis_list = [start_vector / beta]
    for krylov_step in range(ITERS):
        current = basis_list[-1]
        inner = jnp.sum(basis_local * current, axis=1)
        restricted = lax.psum(
            jnp.dot(inner, member_table, precision=highest) * factor, ("sub", "coarse")
        )
        local_part = jnp.einsum(
            "bij,bj->bi", inverse_blocks, current + margin(current), precision=highest
        )
        coarse_part = jnp.dot(coarse_inverse, restricted, precision=highest)
        coarse_full = lax.all_gather(coarse_part, "coarse", axis=0, tiled=True)
        prolonged = jnp.dot(member_table, coarse_full, precision=highest)
        direction = local_part + prolonged[:, None] * basis_local
        directions.append(direction)
        flat_line = direction.reshape(-1)
        link_line = link_local.reshape(-1)
        zero_pad = jnp.zeros((1,), jnp.float32)
        ahead_terms = jnp.concatenate([flat_line[1:], zero_pad]) * link_line
        behind_terms = jnp.concatenate([zero_pad, (link_line * flat_line)[:-1]])
        product = (
            diagonal_local * direction
            - (ahead_terms + behind_terms).reshape(direction.shape)
            - margin(direction)
        )
        projected = lax.psum(
            jnp.stack([jnp.sum(vector * product) for vector in basis_list]), ("sub", "coarse")
        )
        for position in range(len(basis_list)):
            product = product - projected[position] * basis_list[position]
        norm_new = jnp.sqrt(squared_norm(product))
        columns.append([projected[position] for position in range(len(basis_list))] + [norm_new])
        basis_list.append(product / norm_new)
    weights = givens_solve(columns, beta)
    solution = weights[0] * directions[0]
    for position in range(1, ITERS):
        solution = solution + weights[position] * directions[position]
    return solution.reshape(right_side.shape)


def solution(mesh):
    placed = (
        P("sub", "coarse", None, None),
        P("sub", "coarse", None, None),
        P("sub", "coarse", None, None),
        P("sub", "coarse", None, None, None),
        P("sub", "coarse", None, None, None),
        P("sub", "coarse", None, None),
        P("coarse", None),
        P("sub", None),
        P("sub", None),
        P("sub", "coarse", None, None),
        P("sub", "coarse", None),
    )
    return jax.shard_map(
        on_device,
        mesh=mesh,
        in_specs=placed,
        out_specs=P("sub", "coarse", None, None),
        check_vma=False,
    )
```

profile of v0, /device:TPU:0, one launch (start us, length us, event | category | flops | bytes accessed | tf_op | source)
XLA Modules:
  0.0 958.9 jit_solution(15861982066872133460)
XLA Ops:
  2.3 42.2 %psum.91 = f32[]{:T(128)} all-reduce(f32[]{:T(128)} %multiply_reduce_fusion.14), channel_id=1, replica_groups=mesh['sub'=8,'coarse'=4] {'sub','coarse'}, use_global_device_ids=true, to_apply=%region_1.0 | all-reduce | flops 1 | bytes 8 | tf_op jit(solution)/shard_map/psum | solution.py:94
  46.9 10.0 %all_gather.108 = f32[64,128]{1,0:T(8,128)S(1)} all-gather(f32[8,128]{1,0:T(8,128)S(1)} %get-tuple-element.63), channel_id=1, replica_groups=mesh['sub'=8,'coarse'=4] {'sub'}, dimensions={0}, use_global_device_ids=true | all-gather | bytes 36864 | tf_op jit(solution)/shard_map/all_gather | solution.py:82
  87.8 15.4 %fusion.6 = f32[128,1,128]{2,1,0:T(1,128)S(1)} fusion(f32[128,128,1]{1,2,0:T(1,128)S(1)} %bitcast.355, f32[1,1,128,128,128]{4,3,2,1,0:T(8,128)} %param.16), kind=kOutput, calls=%fused_computation.14 | convolution fusion | flops 25165824 | bytes 8519680 | tf_op jit(solution)/shard_map/bij,bj->bi/dot_general | solution.py:107
  103.5 39.4 %psum.92 = f32[512]{0:T(512)S(1)} all-reduce(f32[512]{0:T(512)S(1)} %broadcast_multiply_fusion.3), channel_id=1, replica_groups=mesh['sub'=8,'coarse'=4] {'sub','coarse'}, use_global_device_ids=true, to_apply=%region_3.5 | all-reduce | flops 512 | bytes 4096 | tf_op jit(solution)/shard_map/psum | solution.py:104
  153.9 9.8 %all_gather.113 = f32[64,128]{1,0:T(8,128)S(1)} all-gather(f32[8,128]{1,0:T(8,128)S(1)} %get-tuple-element.59), channel_id=1, replica_groups=mesh['sub'=8,'coarse'=4] {'sub'}, dimensions={0}, use_global_device_ids=true | all-gather | bytes 36864 | tf_op jit(solution)/shard_map/all_gather | solution.py:82
  191.5 37.8 %psum.93 = f32[]{:T(128)} all-reduce(f32[]{:T(128)} %get-tuple-element.80), channel_id=1, replica_groups=mesh['sub'=8,'coarse'=4] {'sub','coarse'}, use_global_device_ids=true, to_apply=%region_5.7 | all-reduce | flops 1 | bytes 8 | tf_op jit(solution)/shard_map/psum | solution.py:125
  230.6 41.2 %psum.94 = f32[]{:T(128)} all-reduce(f32[]{:T(128)} %multiply_reduce_fusion.12), channel_id=1, replica_groups=mesh['sub'=8,'coarse'=4] {'sub','coarse'}, use_global_device_ids=true, to_apply=%region_7.9 | all-reduce | flops 1 | bytes 8 | tf_op jit(solution)/shard_map/psum | solution.py:94
  274.0 10.1 %all_gather.117 = f32[64,128]{1,0:T(8,128)S(1)} all-gather(f32[8,128]{1,0:T(8,128)S(1)} %get-tuple-element.55), channel_id=1, replica_groups=mesh['sub'=8,'coarse'=4] {'sub'}, dimensions={0}, use_global_device_ids=true | all-gather | bytes 36864 | tf_op jit(solution)/shard_map/all_gather | solution.py:82
  311.1 15.4 %fusion.4 = f32[128,1,128]{2,1,0:T(1,128)S(1)} fusion(f32[128,128,1]{1,2,0:T(1,128)S(1)} %bitcast.356, f32[1,1,128,128,128]{4,3,2,1,0:T(8,128)} %param.16), kind=kOutput, calls=%fused_computation.12 | convolution fusion | flops 25165824 | bytes 8519680 | tf_op jit(solution)/shard_map/bij,bj->bi/dot_general | solution.py:107
  326.8 37.7 %psum.95 = f32[512]{0:T(512)S(1)} all-reduce(f32[512]{0:T(512)S(1)} %broadcast_multiply_fusion.2), channel_id=1, replica_groups=mesh['sub'=8,'coarse'=4] {'sub','coarse'}, use_global_device_ids=true, to_apply=%region_9.11 | all-reduce | flops 512 | bytes 4096 | tf_op jit(solution)/shard_map/psum | solution.py:104
  375.4 9.8 %all_gather.122 = f32[64,128]{1,0:T(8,128)S(1)} all-gather(f32[8,128]{1,0:T(8,128)S(1)} %get-tuple-element.51), channel_id=1, replica_groups=mesh['sub'=8,'coarse'=4] {'sub'}, dimensions={0}, use_global_device_ids=true | all-gather | bytes 36864 | tf_op jit(solution)/shard_map/all_gather | solution.py:82
  413.5 37.6 %psum.96 = f32[2]{0:T(128)S(1)} all-reduce(f32[2]{0:T(128)S(1)} %pad_maximum_fusion.8), channel_id=1, replica_groups=mesh['sub'=8,'coarse'=4] {'sub','coarse'}, use_global_device_ids=true, to_apply=%region_12.14 | all-reduce | flops 2 | bytes 16 | tf_op jit(solution)/shard_map/psum | solution.py:125
  453.6 41.7 %psum.97 = f32[]{:T(128)} all-reduce(f32[]{:T(128)} %get-tuple-element.21), channel_id=1, replica_groups=mesh['sub'=8,'coarse'=4] {'sub','coarse'}, use_global_device_ids=true, to_apply=%region_14.16 | all-reduce | flops 1 | bytes 8 | tf_op jit(solution)/shard_map/psum | solution.py:94
  496.8 10.1 %all_gather.126 = f32[64,128]{1,0:T(8,128)S(1)} all-gather(f32[8,128]{1,0:T(8,128)S(1)} %get-tuple-element.47), channel_id=1, replica_groups=mesh['sub'=8,'coarse'=4] {'sub'}, dimensions={0}, use_global_device_ids=true | all-gather | bytes 36864 | tf_op jit(solution)/shard_map/all_gather | solution.py:82
  533.0 15.4 %fusion.2 = f32[128,1,128]{2,1,0:T(1,128)S(1)} fusion(f32[128,128,1]{1,2,0:T(1,128)S(1)} %bitcast.357, f32[1,1,128,128,128]{4,3,2,1,0:T(8,128)} %param.16), kind=kOutput, calls=%fused_computation.10 | convolution fusion | flops 25165824 | bytes 8519680 | tf_op jit(solution)/shard_map/bij,bj->bi/dot_general | solution.py:107
  548.6 37.7 %psum.98 = f32[512]{0:T(512)S(1)} all-reduce(f32[512]{0:T(512)S(1)} %broadcast_multiply_fusion.1), channel_id=1, replica_groups=mesh['sub'=8,'coarse'=4] {'sub','coarse'}, use_global_device_ids=true, to_apply=%region_16.18 | all-reduce | flops 512 | bytes 4096 | tf_op jit(solution)/shard_map/psum | solution.py:104
  597.2 9.8 %all_gather.131 = f32[64,128]{1,0:T(8,128)S(1)} all-gather(f32[8,128]{1,0:T(8,128)S(1)} %get-tuple-element.43), channel_id=1, replica_groups=mesh['sub'=8,'coarse'=4] {'sub'}, dimensions={0}, use_global_device_ids=true | all-gather | bytes 36864 | tf_op jit(solution)/shard_map/all_gather | solution.py:82
  637.2 37.6 %psum.99 = f32[3]{0:T(128)S(1)} all-reduce(f32[3]{0:T(128)S(1)} %pad_maximum_fusion.9), channel_id=1, replica_groups=mesh['sub'=8,'coarse'=4] {'sub','coarse'}, use_global_device_ids=true, to_apply=%region_20.22 | all-reduce | flops 3 | bytes 24 | tf_op jit(solution)/shard_map/psum | solution.py:125
  677.9 40.7 %psum.100 = f32[]{:T(128)} all-reduce(f32[]{:T(128)} %get-tuple-element.17), channel_id=1, replica_groups=mesh['sub'=8,'coarse'=4] {'sub','coarse'}, use_global_device_ids=true, to_apply=%region_22.24 | all-reduce | flops 1 | bytes 8 | tf_op jit(solution)/shard_map/psum | solution.py:94
  720.0 10.0 %all_gather.135 = f32[64,128]{1,0:T(8,128)S(1)} all-gather(f32[8,128]{1,0:T(8,128)S(1)} %get-tuple-element.39), channel_id=1, replica_groups=mesh['sub'=8,'coarse'=4] {'sub'}, dimensions={0}, use_global_device_ids=true | all-gather | bytes 36864 | tf_op jit(solution)/shard_map/all_gather | solution.py:82
  757.1 15.4 %fusion = f32[128,1,128]{2,1,0:T(1,128)S(1)} fusion(f32[128,128,1]{1,2,0:T(1,128)S(1)} %bitcast.358, f32[1,1,128,128,128]{4,3,2,1,0:T(8,128)} %param.16), kind=kOutput, calls=%fused_computation.8 | convolution fusion | flops 25165824 | bytes 8519680 | tf_op jit(solution)/shard_map/bij,bj->bi/dot_general | solution.py:107
  772.7 37.7 %psum.101 = f32[512]{0:T(512)S(1)} all-reduce(f32[512]{0:T(512)S(1)} %broadcast_multiply_fusion), channel_id=1, replica_groups=mesh['sub'=8,'coarse'=4] {'sub','coarse'}, use_global_device_ids=true, to_apply=%region_24.26 | all-reduce | flops 512 | bytes 4096 | tf_op jit(solution)/shard_map/psum | solution.py:104
  860.6 37.6 %psum.102 = f32[4]{0:T(128)S(1)} all-reduce(f32[4]{0:T(128)S(1)} %pad_maximum_fusion.10), channel_id=1, replica_groups=mesh['sub'=8,'coarse'=4] {'sub','coarse'}, use_global_device_ids=true, to_apply=%region_29.31 | all-reduce | flops 4 | bytes 32 | tf_op jit(solution)/shard_map/psum | solution.py:125
  908.5 41.8 %psum.103 = f32[]{:T(128)} all-reduce(f32[]{:T(128)} %multiply_reduce_fusion), channel_id=1, replica_groups=mesh['sub'=8,'coarse'=4] {'sub','coarse'}, use_global_device_ids=true, to_apply=%region_31.33 | all-reduce | flops 1 | bytes 8 | tf_op jit(solution)/shard_map/psum | solution.py:94
  (159 shorter events, 297.0 us)
Async XLA Ops:
  0.0 87.0 %copy-start = (f32[1,1,4,128,128]{4,3,2,1,0:T(8,128)S(1)}, f32[1,1,4,128,128]{4,3,2,1,0:T(8,128)}, u32[]{:S(2)}) copy-start(f32[1,1,4,128,128]{4,3,2,1,0:T(8,128)} %param.17) | copy-start | bytes 786436
  0.0 153.1 %copy-start.1 = (f32[1,1,128,128]{3,2,1,0:T(8,128)S(1)}, f32[1,1,128,128]{3,2,1,0:T(8,128)}, u32[]{:S(2)}) copy-start(f32[1,1,128,128]{3,2,1,0:T(8,128)} %param.18) | copy-start | bytes 196612
  0.0 103.2 %copy-start.5 = (s32[1,1,128]{2,1,0:T(1,128)S(1)}, s32[1,1,128]{2,1,0:T(1,128)}, u32[]{:S(2)}) copy-start(s32[1,1,128]{2,1,0:T(1,128)} %param.23) | copy-start | bytes 1540
  0.0 142.9 %copy-start.2 = (f32[128,512]{1,0:T(8,128)S(1)}, f32[128,512]{1,0:T(8,128)}, u32[]{:S(2)}) copy-start(f32[128,512]{1,0:T(8,128)} %param.19) | copy-start | bytes 786436
  0.0 190.4 %copy-start.3 = (f32[1,1,128,128]{3,2,1,0:T(8,128)S(1)}, f32[1,1,128,128]{3,2,1,0:T(8,128)}, u32[]{:S(2)}) copy-start(f32[1,1,128,128]{3,2,1,0:T(8,128)} %param.15) | copy-start | bytes 196612
  0.0 190.5 %copy-start.4 = (f32[1,1,128,128]{3,2,1,0:T(8,128)S(1)}, f32[1,1,128,128]{3,2,1,0:T(8,128)}, u32[]{:S(2)}) copy-start(f32[1,1,128,128]{3,2,1,0:T(8,128)} %param.14) | copy-start | bytes 196612
where the time goes:
time: 971 us; the launch traced here: 959 us
  blocking collectives  835 us (86%)
  matrix products  73.9 us (8%)
  other arithmetic  21.1 us (2%)
  between operations  20.1 us (2%)
    all_gather x32, blocking collectives, margin(): gathered = lax.all_gather(outgoing[round_id], 'sub', axis=0, tiled=True)  286 us
    psum x5, blocking collectives, squared_norm(): return lax.psum(jnp.sum(values * values), ('sub', 'coarse'))  208 us
    psum x4, blocking collectives, on_device(): lax.psum(jnp.dot(inner, member_table, precision=highest) * factor, ('sub'...  152 us
    psum x4, blocking collectives, on_device(): lax.psum(jnp.stack([jnp.sum(vector * product) for vector in basis_list]),...  151 us
    dot_general x4, matrix products, on_device(): jnp.einsum('bij,bj->bi', inverse_blocks, current + margin(current), preci...  61.5 us
    all_gather x4, blocking collectives, on_device(): coarse_full = lax.all_gather(coarse_part, 'coarse', axis=0, tiled=True)  38.7 us

commit v1 on v0

--- a/solution.py
+++ b/solution.py
@@ -7,6 +7,25 @@
 BPD = 128
 AGG_DEV = 16
 ITERS = 4
+
+
+def joined_along(tiles, dim):
+    lengths = list(tiles.shape[1:])
+    lengths[dim] *= tiles.shape[0]
+    return jnp.moveaxis(tiles, 0, dim).reshape(lengths)
+
+
+def grow_blocks(x, axis):
+    count, index = (lax.axis_size(axis), lax.axis_index(axis))
+    blocks, bit = (x[None], 1)
+    while bit < count:
+        received = lax.ppermute(blocks, axis, [(i, i ^ bit) for i in range(count)])
+        low = index & bit == 0
+        blocks = jnp.concatenate(
+            [jnp.where(low, blocks, received), jnp.where(low, received, blocks)]
+        )
+        bit *= 2
+    return blocks
 
 
 def givens_solve(columns, beta):
@@ -79,7 +98,7 @@
         outgoing = jnp.take(values, blocks.reshape(-1), axis=0).reshape(rounds, widest, unknowns)
         pieces = []
         for round_id in range(rounds):
-            gathered = lax.all_gather(outgoing[round_id], "sub", axis=0, tiled=True)
+            gathered = joined_along(grow_blocks(outgoing[round_id], "sub"), 0)
             pieces.append(lax.dynamic_slice_in_dim(gathered, paired[round_id] * widest, widest, 0))
         incoming = jnp.stack(pieces)
         mapped = (

time: 971 us -> 801 us (0.82)
  blocking collectives: 835 us -> 556 us
  starting transfers between devices: 0 us -> 78.7 us
  waiting for transfers between devices: 0 us -> 25.6 us
    all_gather x32 -> x0, blocking collectives: 286 us -> none  [margin(): gathered = lax.all_gather(outgoing[round_id], 'sub', axis=0, tiled=True)]
    ppermute x0 -> x96, starting transfers between devices: none -> 78.7 us  [grow_blocks(): received = lax.ppermute(blocks, axis, [(i, i ^ bit) for i in range(count)])]
    ppermute x0 -> x96, waiting for transfers between devices: none -> 25.6 us  [grow_blocks(): received = lax.ppermute(blocks, axis, [(i, i ^ bit) for i in range(count)])]
  transfers between devices with their start and end apart: 0 -> 96, of which waited for: 0 -> 39; matrix products, arithmetic and copies ran while one was open for 0% -> 1% of each run, Pallas kernels for 0% -> 0%
where the time goes in v1:
time: 801 us; the launch traced here: 790 us
  blocking collectives  556 us (69%)
  starting transfers between devices  78.7 us (10%)
  matrix products  76.2 us (10%)
  waiting for transfers between devices  25.6 us (3%)
  other arithmetic  22.1 us (3%)
  between operations  21.6 us (3%)
  local copies, waits for them, and re-layouts  9.33 us (1%)
    psum x5, blocking collectives, squared_norm(): return lax.psum(jnp.sum(values * values), ('sub', 'coarse'))  208 us
    psum x4, blocking collectives, on_device(): lax.psum(jnp.dot(inner, member_table, precision=highest) * factor, ('sub'...  157 us
    psum x4, blocking collectives, on_device(): lax.psum(jnp.stack([jnp.sum(vector * product) for vector in basis_list]),...  152 us
    ppermute x96, starting transfers between devices, grow_blocks(): received = lax.ppermute(blocks, axis, [(i, i ^ bit) for i in range(count)])  78.7 us
    dot_general x4, matrix products, on_device(): jnp.einsum('bij,bj->bi', inverse_blocks, current + margin(current), preci...  61.5 us
    all_gather x4, blocking collectives, on_device(): coarse_full = lax.all_gather(coarse_part, 'coarse', axis=0, tiled=True)  38.7 us
    ppermute x96, waiting for transfers between devices, grow_blocks(): received = lax.ppermute(blocks, axis, [(i, i ^ bit) for i in range(count)])  25.6 us
  transfers between devices with their start and end apart: 96, of which 39 were waited for; matrix products, arithmetic and copies ran while one was open for 1% of the time, Pallas kernels for 0%

profile of v1, /device:TPU:0, one launch (start us, length us, event | category | flops | bytes accessed | tf_op | source)
XLA Modules:
  0.0 790.0 jit_solution(880800471064364964)
XLA Ops:
  2.3 42.2 %psum.91 = f32[]{:T(128)} all-reduce(f32[]{:T(128)} %multiply_reduce_fusion.14), channel_id=1, replica_groups=mesh['sub'=8,'coarse'=4] {'sub','coarse'}, use_global_device_ids=true, to_apply=%region_1.0 | all-reduce | flops 1 | bytes 8 | tf_op jit(solution)/shard_map/psum | solution.py:113
  49.6 40.3 %psum.92 = f32[512]{0:T(512)S(1)} all-reduce(f32[512]{0:T(512)S(1)} %broadcast_multiply_fusion.3), channel_id=1, replica_groups=mesh['sub'=8,'coarse'=4] {'sub','coarse'}, use_global_device_ids=true, to_apply=%region_3.5 | all-reduce | flops 512 | bytes 4096 | tf_op jit(solution)/shard_map/psum | solution.py:123
  91.1 9.8 %all-gather = f32[4,1,128]{2,1,0:T(1,128)S(1)} all-gather(f32[1,1,128]{2,1,0:T(1,128)S(1)} %convolution_bitcast_fusion.7), channel_id=1, replica_groups=mesh['sub'=8,'coarse'=4] {'coarse'}, dimensions={0}, use_global_device_ids=true | all-gather | bytes 2560 | tf_op jit(solution)/shard_map/all_gather | solution.py:130
  120.2 15.4 %fusion.6 = f32[128,1,128]{2,1,0:T(1,128)S(1)} fusion(f32[128,128,1]{1,2,0:T(1,128)S(1)} %bitcast.611, f32[1,1,128,128,128]{4,3,2,1,0:T(8,128)} %param.16), kind=kOutput, calls=%fused_computation.14 | convolution fusion | flops 25165824 | bytes 8519680 | tf_op jit(solution)/shard_map/bij,bj->bi/dot_general | solution.py:126
  150.4 37.8 %psum.93 = f32[]{:T(128)} all-reduce(f32[]{:T(128)} %get-tuple-element.320), channel_id=1, replica_groups=mesh['sub'=8,'coarse'=4] {'sub','coarse'}, use_global_device_ids=true, to_apply=%region_5.7 | all-reduce | flops 1 | bytes 8 | tf_op jit(solution)/shard_map/psum | solution.py:144
  189.5 42.5 %psum.94 = f32[]{:T(128)} all-reduce(f32[]{:T(128)} %multiply_reduce_fusion.12), channel_id=1, replica_groups=mesh['sub'=8,'coarse'=4] {'sub','coarse'}, use_global_device_ids=true, to_apply=%region_7.9 | all-reduce | flops 1 | bytes 8 | tf_op jit(solution)/shard_map/psum | solution.py:113
  235.4 38.7 %psum.95 = f32[512]{0:T(512)S(1)} all-reduce(f32[512]{0:T(512)S(1)} %broadcast_multiply_fusion.2), channel_id=1, replica_groups=mesh['sub'=8,'coarse'=4] {'sub','coarse'}, use_global_device_ids=true, to_apply=%region_9.11 | all-reduce | flops 512 | bytes 4096 | tf_op jit(solution)/shard_map/psum | solution.py:123
  274.4 9.6 %all-gather.1 = f32[4,1,128]{2,1,0:T(1,128)S(1)} all-gather(f32[1,1,128]{2,1,0:T(1,128)S(1)} %convolution_bitcast_fusion.5), channel_id=1, replica_groups=mesh['sub'=8,'coarse'=4] {'coarse'}, dimensions={0}, use_global_device_ids=true | all-gather | bytes 2560 | tf_op jit(solution)/shard_map/all_gather | solution.py:130
  299.8 15.4 %fusion.4 = f32[128,1,128]{2,1,0:T(1,128)S(1)} fusion(f32[128,128,1]{1,2,0:T(1,128)S(1)} %bitcast.612, f32[1,1,128,128,128]{4,3,2,1,0:T(8,128)} %param.16), kind=kOutput, calls=%fused_computation.12 | convolution fusion | flops 25165824 | bytes 8519680 | tf_op jit(solution)/shard_map/bij,bj->bi/dot_general | solution.py:126
  332.0 38.1 %psum.96 = f32[2]{0:T(128)S(1)} all-reduce(f32[2]{0:T(128)S(1)} %pad_maximum_fusion.72), channel_id=1, replica_groups=mesh['sub'=8,'coarse'=4] {'sub','coarse'}, use_global_device_ids=true, to_apply=%region_12.14 | all-reduce | flops 2 | bytes 16 | tf_op jit(solution)/shard_map/psum | solution.py:144
  372.6 40.9 %psum.97 = f32[]{:T(128)} all-reduce(f32[]{:T(128)} %get-tuple-element.21), channel_id=1, replica_groups=mesh['sub'=8,'coarse'=4] {'sub','coarse'}, use_global_device_ids=true, to_apply=%region_14.16 | all-reduce | flops 1 | bytes 8 | tf_op jit(solution)/shard_map/psum | solution.py:113
  416.3 39.7 %psum.98 = f32[512]{0:T(512)S(1)} all-reduce(f32[512]{0:T(512)S(1)} %broadcast_multiply_fusion.1), channel_id=1, replica_groups=mesh['sub'=8,'coarse'=4] {'sub','coarse'}, use_global_device_ids=true, to_apply=%region_16.18 | all-reduce | flops 512 | bytes 4096 | tf_op jit(solution)/shard_map/psum | solution.py:123
  456.3 9.7 %all-gather.2 = f32[4,1,128]{2,1,0:T(1,128)S(1)} all-gather(f32[1,1,128]{2,1,0:T(1,128)S(1)} %convolution_bitcast_fusion.3), channel_id=1, replica_groups=mesh['sub'=8,'coarse'=4] {'coarse'}, dimensions={0}, use_global_device_ids=true | all-gather | bytes 2560 | tf_op jit(solution)/shard_map/all_gather | solution.py:130
  482.4 15.4 %fusion.2 = f32[128,1,128]{2,1,0:T(1,128)S(1)} fusion(f32[128,128,1]{1,2,0:T(1,128)S(1)} %bitcast.613, f32[1,1,128,128,128]{4,3,2,1,0:T(8,128)} %param.16), kind=kOutput, calls=%fused_computation.10 | convolution fusion | flops 25165824 | bytes 8519680 | tf_op jit(solution)/shard_map/bij,bj->bi/dot_general | solution.py:126
  514.3 38.0 %psum.99 = f32[3]{0:T(128)S(1)} all-reduce(f32[3]{0:T(128)S(1)} %pad_maximum_fusion.73), channel_id=1, replica_groups=mesh['sub'=8,'coarse'=4] {'sub','coarse'}, use_global_device_ids=true, to_apply=%region_20.22 | all-reduce | flops 3 | bytes 24 | tf_op jit(solution)/shard_map/psum | solution.py:144
  552.9 2.6 multiply_reduce_fusion.5
  555.5 42.0 %psum.100 = f32[]{:T(128)} all-reduce(f32[]{:T(128)} %get-tuple-element.17), channel_id=1, replica_groups=mesh['sub'=8,'coarse'=4] {'sub','coarse'}, use_global_device_ids=true, to_apply=%region_22.24 | all-reduce | flops 1 | bytes 8 | tf_op jit(solution)/shard_map/psum | solution.py:113
  600.3 38.7 %psum.101 = f32[512]{0:T(512)S(1)} all-reduce(f32[512]{0:T(512)S(1)} %broadcast_multiply_fusion), channel_id=1, replica_groups=mesh['sub'=8,'coarse'=4] {'sub','coarse'}, use_global_device_ids=true, to_apply=%region_24.26 | all-reduce | flops 512 | bytes 4096 | tf_op jit(solution)/shard_map/psum | solution.py:123
  639.3 9.6 %all-gather.3 = f32[4,1,128]{2,1,0:T(1,128)S(1)} all-gather(f32[1,1,128]{2,1,0:T(1,128)S(1)} %convolution_bitcast_fusion.1), channel_id=1, replica_groups=mesh['sub'=8,'coarse'=4] {'coarse'}, dimensions={0}, use_global_device_ids=true | all-gather | bytes 2560 | tf_op jit(solution)/shard_map/all_gather | solution.py:130
  666.6 15.4 %fusion = f32[128,1,128]{2,1,0:T(1,128)S(1)} fusion(f32[128,128,1]{1,2,0:T(1,128)S(1)} %bitcast.614, f32[1,1,128,128,128]{4,3,2,1,0:T(8,128)} %param.16), kind=kOutput, calls=%fused_computation.8 | convolution fusion | flops 25165824 | bytes 8519680 | tf_op jit(solution)/shard_map/bij,bj->bi/dot_general | solution.py:126
  697.4 2.7 pad_maximum_fusion.74
  700.1 38.1 %psum.102 = f32[4]{0:T(128)S(1)} all-reduce(f32[4]{0:T(128)S(1)} %pad_maximum_fusion.74), channel_id=1, replica_groups=mesh['sub'=8,'coarse'=4] {'sub','coarse'}, use_global_device_ids=true, to_apply=%region_29.31 | all-reduce | flops 4 | bytes 32 | tf_op jit(solution)/shard_map/psum | solution.py:144
  744.0 3.3 multiply_reduce_fusion
  747.3 40.8 %psum.103 = f32[]{:T(128)} all-reduce(f32[]{:T(128)} %multiply_reduce_fusion), channel_id=1, replica_groups=mesh['sub'=8,'coarse'=4] {'sub','coarse'}, use_global_device_ids=true, to_apply=%region_31.33 | all-reduce | flops 1 | bytes 8 | tf_op jit(solution)/shard_map/psum | solution.py:113
  (485 shorter events, 141.8 us)
Async XLA Ops:
  46.9 58.9 %collective-permute-start = (f32[1,8,128]{2,1,0:T(8,128)S(1)}, f32[1,8,128]{2,1,0:T(8,128)S(1)}, u32[]{:S(2)}, u32[]{:S(2)}) collective-permute-start(f32[1,8,128]{2,1,0:T(8,128)S(1)} %get-tuple-element.297), channel_id=1, source_target_pairs={{0,4},{4,0},{8,12},{12,8},{16,20},{20,16},{24,28},{28,24},{1,5},{5... | collective-permute-start | bytes 12296 | tf_op jit(solution)/shard_map/ppermute | solution.py:22
  46.9 58.9 %collective-permute-start.3 = (f32[1,8,128]{2,1,0:T(8,128)S(1)}, f32[1,8,128]{2,1,0:T(8,128)S(1)}, u32[]{:S(2)}, u32[]{:S(2)}) collective-permute-start(f32[1,8,128]{2,1,0:T(8,128)S(1)} %get-tuple-element.300), channel_id=1, source_target_pairs={{0,4},{4,0},{8,12},{12,8},{16,20},{20,16},{24,28},{28,24},{1,5},{5... | collective-permute-start | bytes 12296 | tf_op jit(solution)/shard_map/ppermute | solution.py:22
  47.4 58.4 %collective-permute-start.6 = (f32[1,8,128]{2,1,0:T(8,128)S(1)}, f32[1,8,128]{2,1,0:T(8,128)S(1)}, u32[]{:S(2)}, u32[]{:S(2)}) collective-permute-start(f32[1,8,128]{2,1,0:T(8,128)S(1)} %get-tuple-element.299), channel_id=1, source_target_pairs={{0,4},{4,0},{8,12},{12,8},{16,20},{20,16},{24,28},{28,24},{1,5},{5... | collective-permute-start | bytes 12296 | tf_op jit(solution)/shard_map/ppermute | solution.py:22
  47.5 58.3 %collective-permute-start.9 = (f32[1,8,128]{2,1,0:T(8,128)S(1)}, f32[1,8,128]{2,1,0:T(8,128)S(1)}, u32[]{:S(2)}, u32[]{:S(2)}) collective-permute-start(f32[1,8,128]{2,1,0:T(8,128)S(1)} %get-tuple-element.298), channel_id=1, source_target_pairs={{0,4},{4,0},{8,12},{12,8},{16,20},{20,16},{24,28},{28,24},{1,5},{5... | collective-permute-start | bytes 12296 | tf_op jit(solution)/shard_map/ppermute | solution.py:22
  105.9 4.5 collective-permute-start.1
  108.3 5.7 collective-permute-start.7
  234.1 52.2 %collective-permute-start.24 = (f32[1,8,128]{2,1,0:T(8,128)S(1)}, f32[1,8,128]{2,1,0:T(8,128)S(1)}, u32[]{:S(2)}, u32[]{:S(2)}) collective-permute-start(f32[1,8,128]{2,1,0:T(8,128)S(1)} %get-tuple-element.261), channel_id=1, source_target_pairs={{0,4},{4,0},{8,12},{12,8},{16,20},{20,16},{24,28},{28,24},{1,5},{5... | collective-permute-start | bytes 12296 | tf_op jit(solution)/shard_map/ppermute | solution.py:22
  234.2 52.2 %collective-permute-start.27 = (f32[1,8,128]{2,1,0:T(8,128)S(1)}, f32[1,8,128]{2,1,0:T(8,128)S(1)}, u32[]{:S(2)}, u32[]{:S(2)}) collective-permute-start(f32[1,8,128]{2,1,0:T(8,128)S(1)} %get-tuple-element.264), channel_id=1, source_target_pairs={{0,4},{4,0},{8,12},{12,8},{16,20},{20,16},{24,28},{28,24},{1,5},{5... | collective-permute-start | bytes 12296 | tf_op jit(solution)/shard_map/ppermute | solution.py:22
  234.7 51.7 %collective-permute-start.30 = (f32[1,8,128]{2,1,0:T(8,128)S(1)}, f32[1,8,128]{2,1,0:T(8,128)S(1)}, u32[]{:S(2)}, u32[]{:S(2)}) collective-permute-start(f32[1,8,128]{2,1,0:T(8,128)S(1)} %get-tuple-element.263), channel_id=1, source_target_pairs={{0,4},{4,0},{8,12},{12,8},{16,20},{20,16},{24,28},{28,24},{1,5},{5... | collective-permute-start | bytes 12296 | tf_op jit(solution)/shard_map/ppermute | solution.py:22
  234.7 51.7 %collective-permute-start.33 = (f32[1,8,128]{2,1,0:T(8,128)S(1)}, f32[1,8,128]{2,1,0:T(8,128)S(1)}, u32[]{:S(2)}, u32[]{:S(2)}) collective-permute-start(f32[1,8,128]{2,1,0:T(8,128)S(1)} %get-tuple-element.262), channel_id=1, source_target_pairs={{0,4},{4,0},{8,12},{12,8},{16,20},{20,16},{24,28},{28,24},{1,5},{5... | collective-permute-start | bytes 12296 | tf_op jit(solution)/shard_map/ppermute | solution.py:22
  286.4 4.5 collective-permute-start.25
  288.9 5.1 collective-permute-start.31
  290.9 5.3 collective-permute-start.26
  415.0 53.9 %collective-permute-start.48 = (f32[1,8,128]{2,1,0:T(8,128)S(1)}, f32[1,8,128]{2,1,0:T(8,128)S(1)}, u32[]{:S(2)}, u32[]{:S(2)}) collective-permute-start(f32[1,8,128]{2,1,0:T(8,128)S(1)} %get-tuple-element.225), channel_id=1, source_target_pairs={{0,4},{4,0},{8,12},{12,8},{16,20},{20,16},{24,28},{28,24},{1,5},{5... | collective-permute-start | bytes 12296 | tf_op jit(solution)/shard_map/ppermute | solution.py:22
  415.1 53.9 %collective-permute-start.51 = (f32[1,8,128]{2,1,0:T(8,128)S(1)}, f32[1,8,128]{2,1,0:T(8,128)S(1)}, u32[]{:S(2)}, u32[]{:S(2)}) collective-permute-start(f32[1,8,128]{2,1,0:T(8,128)S(1)} %get-tuple-element.228), channel_id=1, source_target_pairs={{0,4},{4,0},{8,12},{12,8},{16,20},{20,16},{24,28},{28,24},{1,5},{5... | collective-permute-start | bytes 12296 | tf_op jit(solution)/shard_map/ppermute | solution.py:22
  415.6 53.4 %collective-permute-start.54 = (f32[1,8,128]{2,1,0:T(8,128)S(1)}, f32[1,8,128]{2,1,0:T(8,128)S(1)}, u32[]{:S(2)}, u32[]{:S(2)}) collective-permute-start(f32[1,8,128]{2,1,0:T(8,128)S(1)} %get-tuple-element.227), channel_id=1, source_target_pairs={{0,4},{4,0},{8,12},{12,8},{16,20},{20,16},{24,28},{28,24},{1,5},{5... | collective-permute-start | bytes 12296 | tf_op jit(solution)/shard_map/ppermute | solution.py:22
  415.6 53.3 %collective-permute-start.57 = (f32[1,8,128]{2,1,0:T(8,128)S(1)}, f32[1,8,128]{2,1,0:T(8,128)S(1)}, u32[]{:S(2)}, u32[]{:S(2)}) collective-permute-start(f32[1,8,128]{2,1,0:T(8,128)S(1)} %get-tuple-element.226), channel_id=1, source_target_pairs={{0,4},{4,0},{8,12},{12,8},{16,20},{20,16},{24,28},{28,24},{1,5},{5... | collective-permute-start | bytes 12296 | tf_op jit(solution)/shard_map/ppermute | solution.py:22
  469.0 4.5 collective-permute-start.49
  599.0 54.2 %collective-permute-start.72 = (f32[1,8,128]{2,1,0:T(8,128)S(1)}, f32[1,8,128]{2,1,0:T(8,128)S(1)}, u32[]{:S(2)}, u32[]{:S(2)}) collective-permute-start(f32[1,8,128]{2,1,0:T(8,128)S(1)} %get-tuple-element.189), channel_id=1, source_target_pairs={{0,4},{4,0},{8,12},{12,8},{16,20},{20,16},{24,28},{28,24},{1,5},{5... | collective-permute-start | bytes 12296 | tf_op jit(solution)/shard_map/ppermute | solution.py:22
  599.0 54.1 %collective-permute-start.75 = (f32[1,8,128]{2,1,0:T(8,128)S(1)}, f32[1,8,128]{2,1,0:T(8,128)S(1)}, u32[]{:S(2)}, u32[]{:S(2)}) collective-permute-start(f32[1,8,128]{2,1,0:T(8,128)S(1)} %get-tuple-element.192), channel_id=1, source_target_pairs={{0,4},{4,0},{8,12},{12,8},{16,20},{20,16},{24,28},{28,24},{1,5},{5... | collective-permute-start | bytes 12296 | tf_op jit(solution)/shard_map/ppermute | solution.py:22
  599.5 53.7 %collective-permute-start.78 = (f32[1,8,128]{2,1,0:T(8,128)S(1)}, f32[1,8,128]{2,1,0:T(8,128)S(1)}, u32[]{:S(2)}, u32[]{:S(2)}) collective-permute-start(f32[1,8,128]{2,1,0:T(8,128)S(1)} %get-tuple-element.191), channel_id=1, source_target_pairs={{0,4},{4,0},{8,12},{12,8},{16,20},{20,16},{24,28},{28,24},{1,5},{5... | collective-permute-start | bytes 12296 | tf_op jit(solution)/shard_map/ppermute | solution.py:22
  599.6 53.6 %collective-permute-start.81 = (f32[1,8,128]{2,1,0:T(8,128)S(1)}, f32[1,8,128]{2,1,0:T(8,128)S(1)}, u32[]{:S(2)}, u32[]{:S(2)}) collective-permute-start(f32[1,8,128]{2,1,0:T(8,128)S(1)} %get-tuple-element.190), channel_id=1, source_target_pairs={{0,4},{4,0},{8,12},{12,8},{16,20},{20,16},{24,28},{28,24},{1,5},{5... | collective-permute-start | bytes 12296 | tf_op jit(solution)/shard_map/ppermute | solution.py:22
  655.7 5.1 collective-permute-start.79
  657.7 5.3 collective-permute-start.74
  (78 other events, 1294.0 us)
